TPU v7x, 32 devices: a whole 2x2x4 slice. The times are simulated.
32 devices in a mesh: groups: 2 (over x), ep: 16 (over z, y, core).
Axes of the slice: x: 2, y: 2, z: 4, core: 2. Of those that a mesh axis runs over, the one named last changes fastest.
Arguments:
- tokens: bfloat16 [1024, 3584], P(('groups', 'ep')), parts along dimension 0, may hold values from -6 to 6
- routes: int32 [1024, 8], P(('groups', 'ep')), parts along dimension 0, may hold values from 0 to 255, all different within a row; in each aligned block of 32 rows (0 to 31, 32 to 63, ...) at most 2 rows name the same one
- gate_num: int32 [1024, 8], P(('groups', 'ep')), parts along dimension 0, may hold values from 1 to 255
- w_gate: bfloat16 [16, 3584, 512], P('ep'), may hold values from -0.09375 to 0.09375
- w_up: bfloat16 [16, 3584, 512], P('ep'), may hold values from -0.09375 to 0.09375
- w_down: bfloat16 [16, 512, 3584], P('ep'), may hold values from -0.1875 to 0.1875
Outputs:
- combined: bfloat16 [1024, 3584], P(('groups', 'ep')), parts along dimension 0
There are 2 independent parts, one for each index of `groups`. A program takes and returns all parts, laid end to end along the dimension named above; an argument that names none is the same for every part. Nothing has to cross between parts.
Inputs may be any that keep to these rules, and one draw needn't show every extreme that they name: `routes`: each row names 8 different experts; among the 32 rows of one device no expert is named more than 2 times, a bound that some block reaches.
All inputs are finite; a program needn't handle non-finite values.
Results may differ from a plain program's by a relative error of at most 0.0058.
Values may be sent and summed in bfloat16 or wider, within the bound.
No kernel may reach another device: no remote copies, remote signals or barrier semaphores. Data moves between devices by JAX's collectives and lax.ppermute only.
A program may use at most 64 MiB of HBM per device.

v0:
```python
import jax
import jax.numpy as jnp
from jax import lax
from jax.sharding import PartitionSpec as P

SPLIT = 2
EXPERTS = 256


def partner_2(block, axis, apart):
    count = lax.axis_size(axis)
    route = []
    for low in range(count):
        high = low | 1 << apart
        if high != low and high < count:
            route += [(low, high), (high, low)]
    return lax.ppermute(block, axis, route)


def expert_mlp(received, w_gate, w_up, w_down):
    local_count = w_gate.shape[0]
    senders = received.shape[0] // local_count
    slot_count = received.shape[1]
    feature_width = received.shape[2]
    blocks = received.reshape(senders, local_count, slot_count, feature_width)
    gate_part = jnp.einsum("secd,edf->secf", blocks, w_gate, preferred_element_type=jnp.float32)
    up_part = jnp.einsum("secd,edf->secf", blocks, w_up, preferred_element_type=jnp.float32)
    hidden = (jax.nn.silu(gate_part) * up_part).astype(jnp.bfloat16)
    output = jnp.einsum("secf,efd->secd", hidden, w_down, preferred_element_type=jnp.float32)
    return output.reshape(senders * local_count, slot_count, feature_width)


def serve_rows(received, w_gate, w_up, w_down):
    parity = lax.axis_index("ep") % 2
    partner = partner_2(received, "ep", 0)
    lower_rows = jnp.where(parity == 0, received, partner)
    upper_rows = jnp.where(parity == 0, partner, received)
    whole_rows = jnp.concatenate([lower_rows, upper_rows], axis=2)
    results = expert_mlp(whole_rows, w_gate, w_up, w_down)
    half_width = results.shape[2] // 2
    lower_out = results[:, :, :half_width]
    upper_out = results[:, :, half_width:]
    kept = jnp.where(parity == 0, lower_out, upper_out)
    sending = jnp.where(parity == 0, upper_out, lower_out)
    arrived = partner_2(sending, "ep", 0)
    summed = (kept + arrived).astype(jnp.bfloat16)
    return lax.all_to_all(summed, "ep", split_axis=0, concat_axis=0, tiled=True)


def shards(tokens, routes, gate_num, w_gate, w_up, w_down):
    tok_rows, top_count = routes.shape
    feature_width = tokens.shape[1]
    devices_all = lax.axis_size("ep")
    experts_all = devices_all // SPLIT
    capacity = max(2, min(tok_rows, 5 * tok_rows * top_count // (2 * EXPERTS)))
    flat_routes = routes.reshape(-1)
    served = flat_routes < experts_all
    one_hot = (flat_routes[:, None] == jnp.arange(experts_all, dtype=jnp.int32)[None, :]).astype(
        jnp.int32
    )
    before = jnp.cumsum(one_hot, axis=0) - one_hot
    position = jnp.sum(before * one_hot, axis=1)
    slot_total = experts_all * capacity
    slot_index = jnp.where(served, flat_routes * capacity + position, slot_total)
    token_of = jnp.arange(tok_rows * top_count, dtype=jnp.int32) // top_count
    source_row = jnp.zeros((slot_total,), jnp.int32).at[slot_index].set(token_of, mode="drop")
    filled = jnp.zeros((slot_total,), jnp.bool_).at[slot_index].set(True, mode="drop")
    outgoing = jnp.where(filled[:, None], tokens[source_row], jnp.zeros((), tokens.dtype))
    outgoing = outgoing.reshape(experts_all, capacity, feature_width)
    half_width = feature_width // SPLIT
    outgoing = outgoing.reshape(experts_all, capacity, SPLIT, half_width)
    outgoing = outgoing.transpose(0, 2, 1, 3).reshape(experts_all * SPLIT, capacity, half_width)
    received = lax.all_to_all(outgoing, "ep", split_axis=0, concat_axis=0, tiled=True)
    returned = serve_rows(received, w_gate, w_up, w_down)
    returned = returned.reshape(experts_all, SPLIT, capacity, half_width)
    expert_rows = returned.transpose(0, 2, 1, 3).reshape(experts_all, capacity, feature_width)
    safe_route = jnp.where(served, flat_routes, 0)
    picked = expert_rows[safe_route, position]
    picked = picked.reshape(tok_rows, top_count, feature_width)
    gate_real = jnp.where(
        served.reshape(tok_rows, top_count), gate_num.astype(jnp.float32) / 256.0, 0.0
    )
    weights = gate_real.astype(jnp.bfloat16)
    combined = jnp.einsum("tk,tkd->td", weights, picked, preferred_element_type=jnp.float32)
    return combined.astype(jnp.bfloat16)


def solution(mesh):
    return jax.shard_map(
        shards,
        mesh=mesh,
        in_specs=(
            P(("groups", "ep"), None),
            P(("groups", "ep"), None),
            P(("groups", "ep"), None),
            P("ep", None, None),
            P("ep", None, None),
            P("ep", None, None),
        ),
        out_specs=P(("groups", "ep"), None),
        check_vma=False,
    )
```

profile of v0, /device:TPU:0, one launch (start us, length us, event | category | flops | bytes accessed | tf_op | source)
XLA Modules:
  0.0 48.8 jit_solution(16190040157651471799)
XLA Ops:
  0.0 0.0 copy-start
  0.0 0.8 %copy.16 = s32[32,8]{1,0:T(8,128)S(1)} copy(s32[32,8]{0,1:T(8,128)} %param.7) | data formatting | bytes 2048 | tf_op args[1]
  0.8 0.1 eq.38
  0.9 0.1 eq.34
  1.0 0.1 reshape.134
  1.1 0.6 %reduce-window.6 = s32[8,2,128]{2,0,1:T(8,128)S(1)} reduce-window(s32[8,2,128]{2,0,1:T(8,128)S(1)} %fusion.22, s32[]{:T(128)} %constant.50.clone.1), window={size=1x1x128 pad=0_0x0_0x127_0}, to_apply=%region_0.0 | reduce-window | flops 260096 | bytes 16388 | tf_op jit(solution)/shard_map/reduce-window
  1.7 0.2 slice_reduce_fusion
  1.9 0.1 fusion.21
  2.0 1.4 %scatter_custom_fusion.1 = s32[16]{0:T(128)S(1)} fusion(s32[256]{0:T(256)S(1)} %bitcast.73, s32[256]{0:T(256)S(1)} %and_select_fusion, s32[]{:T(128)} %constant.50.clone.1), kind=kCustom, calls=%fused_computation.52 | custom fusion | bytes 68 | tf_op jit(solution)/shard_map/scatter | solution.py:66
  3.5 1.5 %scatter_custom_fusion = pred[16]{0:T(512)(128)(4,1)S(1)} fusion(s32[256]{0:T(256)S(1)} %bitcast.74, pred[256]{0:T(512)(128)(4,1)S(1)} %broadcast.151, pred[]{:T(512)} %constant.53.clone.1), kind=kCustom, calls=%fused_computation.50 | custom fusion | bytes 17 | tf_op jit(solution)/shard_map/scatter | solution.py:67
  5.0 0.1 broadcast_in_dim.38
  5.1 0.0 copy-done
  5.1 0.6 %gather_fusion = bf16[16,3584]{1,0:T(8,128)(2,1)S(1)} fusion(bf16[32,3584]{1,0:T(8,128)(2,1)S(1)} %copy-done, s32[1024]{0:T(1024)S(1)} %pad_clamp_fusion), kind=kCustom, calls=%fused_computation | custom fusion | bytes 229440 | tf_op jit(solution)/shard_map/gather | solution.py:68
  5.7 0.2 fusion.14
  5.9 0.1 copy.19
  6.0 14.9 %all_to_all.10 = bf16[16,2,1792]{2,1,0:T(2,128)(2,1)S(1)} all-to-all(bf16[16,2,1792]{2,1,0:T(2,128)(2,1)S(1)} %bitcast.70), channel_id=1, replica_groups=mesh['groups'=2,'ep'=16] {'ep'}, dimensions={0} | all-to-all | bytes 229376 | tf_op jit(solution)/shard_map/all_to_all | solution.py:73
  20.9 0.1 collective-permute-start
  21.0 1.3 %collective-permute-done = bf16[16,2,1792]{2,0,1:T(8,128)(2,1)S(1)} collective-permute-done((bf16[16,2,1792]{2,0,1:T(8,128)(2,1)S(1)}, bf16[16,2,1792]{2,0,1:T(8,128)(2,1)S(1)}, u32[]{:S(2)}, u32[]{:S(2)}) %collective-permute-start) | collective-permute-done | bytes 114720 | tf_op jit(solution)/shard_map/ppermute | solution.py:17
  22.3 2.8 %fusion.8 = f32[16,1,2,512]{3,0,2,1:T(8,128)S(1)} fusion(bf16[1,3584,512]{2,1,0:T(8,128)(2,1)} %param.9, bf16[16,2,1792]{2,0,1:T(8,128)(2,1)S(1)} %get-tuple-element.6, bf16[16,2,1792]{2,0,1:T(8,128)(2,1)S(1)} %get-tuple-element.5), kind=kOutput, calls=%fused_computation.12 | convolution fusion | flops 117899264 | bytes 3964928 | tf_op jit(solution)/shard_map/secd,edf->secf/dot_general | solution.py:26
  25.1 0.0 copy-start.1
  25.1 0.0 copy-start.2
  25.1 4.6 %fusion = f32[16,2,3584]{2,0,1:T(8,128)S(1)} fusion(bf16[1,512,3584]{2,1,0:T(8,128)(2,1)} %param.11, f32[16,1,2,512]{3,0,2,1:T(8,128)S(1)} %fusion.8, bf16[1,3584,512]{2,1,0:T(8,128)(2,1)} %param.10, bf16[16,2,1792]{2,0,1:T(8,128)(2,1)S(1)} %get-tuple-element.6, bf16[16,2,1792]{2,0,1:T(8,128)(2,1)S(1)} %get-tuple-element.5), kind=kOutput, calls=%fused_computation.4 | convolution fusion | flops 235438080 | bytes 8093696 | tf_op jit(solution)/shard_map/secf,efd->secd/dot_general | solution.py:29
  29.7 0.2 collective-permute-start.1
  29.9 1.3 %collective-permute-done.1 = f32[16,2,1792]{2,0,1:T(8,128)S(1)} collective-permute-done((f32[16,2,1792]{2,0,1:T(8,128)S(1)}, f32[16,2,1792]{2,0,1:T(8,128)S(1)}, u32[]{:S(2)}, u32[]{:S(2)}) %collective-permute-start.1) | collective-permute-done | bytes 229408 | tf_op jit(solution)/shard_map/ppermute | solution.py:17
  31.3 0.7 %copy.23 = bf16[16,2,1792]{2,1,0:T(2,128)(2,1)} copy(bf16[16,2,1792]{2,0,1:T(8,128)(2,1)S(1)} %add_convert_fusion) | data formatting | bytes 229376 | tf_op jit(solution)/shard_map/convert_element_type | solution.py:46
  32.0 3.5 %all-to-all-start.1 = ((bf16[16,2,1792]{2,1,0:T(2,128)(2,1)}), bf16[16,2,1792]{2,1,0:T(2,128)(2,1)S(1)}, u32[]{:S(2)}, u32[]{:S(2)}) async-start(bf16[16,2,1792]{2,1,0:T(2,128)(2,1)} %copy.23), calls=%async_computation.1 | async-start | bytes 229376 | tf_op jit(solution)/shard_map/all_to_all | solution.py:47
  35.6 0.0 copy-done.1
  35.6 0.0 copy-done.2
  35.6 0.1 copy.25
  35.7 7.5 %all-to-all-done.1 = bf16[16,2,1792]{2,1,0:T(2,128)(2,1)S(1)} async-done(((bf16[16,2,1792]{2,1,0:T(2,128)(2,1)}), bf16[16,2,1792]{2,1,0:T(2,128)(2,1)S(1)}, u32[]{:S(2)}, u32[]{:S(2)}) %all-to-all-start.1) | async-done | bytes 114720 | tf_op jit(solution)/shard_map/all_to_all | solution.py:47
  43.2 0.1 copy.32
  43.3 0.1 reshape.142
  43.3 4.1 %gather_fusion.1 = bf16[256,3584]{1,0:T(8,128)(2,1)S(1)} fusion(bf16[8,2,3584]{2,1,0:T(2,128)(2,1)S(1)} %reshape.142, s32[256]{0:T(256)S(1)} %bitcast.68), kind=kCustom, calls=%fused_computation.1 | custom fusion | bytes 3672064 | tf_op jit(solution)/shard_map/gather | solution.py:78
  47.5 0.6 %fusion.6 = bf16[32,1,3584]{2,1,0:T(2,128)(2,1)S(1)} fusion(bf16[32,8,1]{1,2,0:T(2,128)(2,1)S(1)} %copy.25, bf16[256,3584]{1,0:T(8,128)(2,1)S(1)} %gather_fusion.1), kind=kOutput, calls=%fused_computation.10 | convolution fusion | flops 1835008 | bytes 2064896 | tf_op jit(solution)/shard_map/tk,tkd->td/dot_general | solution.py:84
  48.1 0.7 %copy.31 = bf16[32,1,3584]{2,0,1:T(8,128)(2,1)} copy(bf16[32,1,3584]{2,1,0:T(2,128)(2,1)S(1)} %fusion.6) | data formatting | bytes 458752 | tf_op jit(solution)/shard_map/tk,tkd->td/dot_general | solution.py:84
  (14 shorter events, 0.2 us)
Async XLA Ops:
  0.0 5.1 %copy-start = (bf16[32,3584]{1,0:T(8,128)(2,1)S(1)}, bf16[32,3584]{1,0:T(8,128)(2,1)}, u32[]{:S(2)}) copy-start(bf16[32,3584]{1,0:T(8,128)(2,1)} %param.6) | copy-start | bytes 688132
  20.9 1.4 %collective-permute-start = (bf16[16,2,1792]{2,0,1:T(8,128)(2,1)S(1)}, bf16[16,2,1792]{2,0,1:T(8,128)(2,1)S(1)}, u32[]{:S(2)}, u32[]{:S(2)}) collective-permute-start(bf16[16,2,1792]{2,0,1:T(8,128)(2,1)S(1)} %copy.21), channel_id=1, source_target_pairs={{0,1},{1,0},{2,3},{3,2},{4,5},{5,4},{6,7},{7,6},{8,9},{9,8},{10,11... | collective-permute-start | bytes 344072 | tf_op jit(solution)/shard_map/ppermute | solution.py:17
  25.1 10.5 %copy-start.1 = (s32[32,8]{0,1:T(8,128)S(1)}, s32[32,8]{0,1:T(8,128)}, u32[]{:S(2)}) copy-start(s32[32,8]{0,1:T(8,128)} %param.7) | copy-start | bytes 3076
  25.1 10.5 %copy-start.2 = (s32[32,8]{0,1:T(8,128)S(1)}, s32[32,8]{0,1:T(8,128)}, u32[]{:S(2)}) copy-start(s32[32,8]{0,1:T(8,128)} %param.8) | copy-start | bytes 3076
  29.7 1.6 %collective-permute-start.1 = (f32[16,2,1792]{2,0,1:T(8,128)S(1)}, f32[16,2,1792]{2,0,1:T(8,128)S(1)}, u32[]{:S(2)}, u32[]{:S(2)}) collective-permute-start(f32[16,2,1792]{2,0,1:T(8,128)S(1)} %slice_select_fusion), channel_id=1, source_target_pairs={{0,1},{1,0},{2,3},{3,2},{4,5},{5,4},{6,7},{7,6},{8,9},{9,8},{10,11... | collective-permute-start | bytes 688136 | tf_op jit(solution)/shard_map/ppermute | solution.py:17
  32.0 11.1 %all-to-all-start.1 = ((bf16[16,2,1792]{2,1,0:T(2,128)(2,1)}), bf16[16,2,1792]{2,1,0:T(2,128)(2,1)S(1)}, u32[]{:S(2)}, u32[]{:S(2)}) async-start(bf16[16,2,1792]{2,1,0:T(2,128)(2,1)} %copy.23), calls=%async_computation.1 | async-start | bytes 229376 | tf_op jit(solution)/shard_map/all_to_all | solution.py:47
where the time goes:
time: 49.1 us; the launch traced here: 48.8 us
  blocking collectives  14.9 us (30%)
  local copies, waits for them, and re-layouts  10.9 us (22%)
  waiting for transfers between devices  10.1 us (21%)
  matrix products  7.98 us (16%)
  starting transfers between devices  3.8 us (8%)
  other arithmetic  1.01 us (2%)
    all_to_all x1, blocking collectives, shards(): lax.all_to_all(outgoing, 'ep', split_axis=0, concat_axis=0, tiled=True)  14.9 us
    all_to_all x1, waiting for transfers between devices, serve_rows(): return lax.all_to_all(summed, 'ep', split_axis=0, concat_axis=0, tiled=True)  7.48 us
    dot_general x1, matrix products, expert_mlp(): jnp.einsum('secf,efd->secd', hidden, w_down, preferred_element_type=jnp.f...  4.61 us
    gather x1, local copies, waits for them, and re-layouts, shards(): picked = expert_rows[safe_route, position]  4.12 us
    all_to_all x1, starting transfers between devices, serve_rows(): return lax.all_to_all(summed, 'ep', split_axis=0, concat_axis=0, tiled=True)  3.51 us
    dot_general x1, matrix products, expert_mlp(): jnp.einsum('secd,edf->secf', blocks, w_gate, preferred_element_type=jnp.f...  2.76 us
    ppermute x2, waiting for transfers between devices, partner_2(): return lax.ppermute(block, axis, route)  2.64 us
    scatter x1, local copies, waits for them, and re-layouts, shards(): jnp.zeros((slot_total,), jnp.bool_).at[slot_index].set(True, mode='drop')  1.49 us
  transfers between devices with their start and end apart: 3, of which 3 were waited for; matrix products, arithmetic and copies ran while one was open for 0% of the time, Pallas kernels for 0%

commit v1 on v0

--- a/solution.py
+++ b/solution.py
@@ -70,7 +70,21 @@
     half_width = feature_width // SPLIT
     outgoing = outgoing.reshape(experts_all, capacity, SPLIT, half_width)
     outgoing = outgoing.transpose(0, 2, 1, 3).reshape(experts_all * SPLIT, capacity, half_width)
-    received = lax.all_to_all(outgoing, "ep", split_axis=0, concat_axis=0, tiled=True)
+    all_values = lax.axis_size("ep")
+    current_arr, z = (all_values, lax.axis_index("ep"))
+    outer = list(outgoing.shape)
+    t1 = outgoing.shape[0] // current_arr
+    outer[0] = t1
+    piece_out = outer[0]
+    outer[0] = piece_out * current_arr
+    received = jnp.zeros(outer, outgoing.dtype)
+    for d in [*range(current_arr)]:
+        lower = lax.dynamic_slice_in_dim(outgoing, (z ^ d) * t1, t1, axis=0)
+        if d:
+            lower = lax.ppermute(
+                lower, axis_name="ep", perm=[(hop_no, hop_no ^ d) for hop_no in range(current_arr)]
+            )
+        received = lax.dynamic_update_slice_in_dim(received, lower, (z ^ d) * piece_out, axis=0)
     returned = serve_rows(received, w_gate, w_up, w_down)
     returned = returned.reshape(experts_all, SPLIT, capacity, half_width)
     expert_rows = returned.transpose(0, 2, 1, 3).reshape(experts_all, capacity, feature_width)

time: 49.1 us -> 62.2 us (1.27)
  starting transfers between devices: 3.8 us -> 25.8 us
  blocking collectives: 14.9 us -> 0 us
  waiting for transfers between devices: 10.1 us -> 13.4 us
  local copies, waits for them, and re-layouts: 10.9 us -> 13.3 us
    ppermute x0 -> x15, starting transfers between devices: none -> 21.9 us  [shards(): lax.ppermute(lower, axis_name='ep', perm=[(hop_no, hop_no ^ d) for hop_no...]
    all_to_all x1 -> x0, blocking collectives: 14.9 us -> none  [shards(): lax.all_to_all(outgoing, 'ep', split_axis=0, concat_axis=0, tiled=True)]
    ppermute x0 -> x15, waiting for transfers between devices: none -> 3.4 us  [shards(): lax.ppermute(lower, axis_name='ep', perm=[(hop_no, hop_no ^ d) for hop_no...]
    dynamic_update_slice x0 -> x16, local copies, waits for them, and re-layouts: none -> 2.01 us  [shards(): lax.dynamic_update_slice_in_dim(received, lower, (z ^ d) * piece_out, axi...]
  transfers between devices with their start and end apart: 3 -> 18, of which waited for: 3 -> 5; matrix products, arithmetic and copies ran while one was open for 0% -> 3% of each run, Pallas kernels for 0% -> 0%
where the time goes in v1:
time: 62.2 us; the launch traced here: 62 us
  starting transfers between devices  25.8 us (41%)
  waiting for transfers between devices  13.4 us (22%)
  local copies, waits for them, and re-layouts  13.3 us (21%)
  matrix products  7.98 us (13%)
  other arithmetic  1.03 us (2%)
    ppermute x15, starting transfers between devices, shards(): lax.ppermute(lower, axis_name='ep', perm=[(hop_no, hop_no ^ d) for hop_no...  21.9 us
    all_to_all x1, waiting for transfers between devices, serve_rows(): return lax.all_to_all(summed, 'ep', split_axis=0, concat_axis=0, tiled=True)  7.48 us
    dot_general x1, matrix products, expert_mlp(): jnp.einsum('secf,efd->secd', hidden, w_down, preferred_element_type=jnp.f...  4.61 us
    gather x1, local copies, waits for them, and re-layouts, shards(): picked = expert_rows[safe_route, position]  4.12 us
    all_to_all x1, starting transfers between devices, serve_rows(): return lax.all_to_all(summed, 'ep', split_axis=0, concat_axis=0, tiled=True)  3.51 us
    ppermute x15, waiting for transfers between devices, shards(): lax.ppermute(lower, axis_name='ep', perm=[(hop_no, hop_no ^ d) for hop_no...  3.4 us
    dot_general x1, matrix products, expert_mlp(): jnp.einsum('secd,edf->secf', blocks, w_gate, preferred_element_type=jnp.f...  2.76 us
    ppermute x2, waiting for transfers between devices, partner_2(): return lax.ppermute(block, axis, route)  2.55 us
  transfers between devices with their start and end apart: 18, of which 5 were waited for; matrix products, arithmetic and copies ran while one was open for 3% of the time, Pallas kernels for 0%

profile of v1, /device:TPU:0, one launch (start us, length us, event | category | flops | bytes accessed | tf_op | source)
XLA Modules:
  0.0 62.0 jit_solution(7883498515940150093)
XLA Ops:
  0.0 0.8 %copy.16 = s32[32,8]{1,0:T(8,128)S(1)} copy(s32[32,8]{0,1:T(8,128)} %param.7) | data formatting | bytes 2048 | tf_op args[1]
  0.8 0.1 eq.38
  0.9 0.1 eq.34
  1.0 0.1 reshape.134
  1.1 0.6 reduce-window.6
  1.7 0.2 slice_reduce_fusion
  1.9 0.1 fusion.21
  2.0 1.4 %scatter_custom_fusion.1 = s32[16]{0:T(128)S(1)} fusion(s32[256]{0:T(256)S(1)} %bitcast.73, s32[256]{0:T(256)S(1)} %and_select_fusion, s32[]{:T(128)} %constant.30.clone.1), kind=kCustom, calls=%fused_computation.68 | custom fusion | bytes 68 | tf_op jit(solution)/shard_map/scatter | solution.py:66
  3.5 1.5 %scatter_custom_fusion = pred[16]{0:T(512)(128)(4,1)S(1)} fusion(s32[256]{0:T(256)S(1)} %bitcast.74, pred[256]{0:T(512)(128)(4,1)S(1)} %broadcast.154, pred[]{:T(512)} %constant.34.clone.1), kind=kCustom, calls=%fused_computation.66 | custom fusion | bytes 17 | tf_op jit(solution)/shard_map/scatter | solution.py:67
  5.0 0.1 broadcast_in_dim.42
  5.1 0.1 copy.19
  5.2 0.6 gather_fusion
  5.8 0.2 fusion.14
  6.1 0.4 constant_dynamic-slice_fusion
  6.5 5.1 %collective-permute-start.9 = (bf16[1,2,1792]{2,0,1:T(2,128)(2,1)S(1)}, bf16[1,2,1792]{2,0,1:T(2,128)(2,1)S(1)}, u32[]{:S(2)}, u32[]{:S(2)}) collective-permute-start(bf16[1,2,1792]{2,0,1:T(2,128)(2,1)S(1)} %get-tuple-element.12), channel_id=1, source_target_pairs={{0,10},{1,11},{2,8},{3,9},{4,14},{5,15},{6,12},{7,13},{8,2},{9,3},... | collective-permute-start | bytes 21512 | tf_op jit(solution)/shard_map/ppermute | solution.py:84
  11.6 2.1 %collective-permute-start.7 = (bf16[1,2,1792]{2,0,1:T(2,128)(2,1)S(1)}, bf16[1,2,1792]{2,0,1:T(2,128)(2,1)S(1)}, u32[]{:S(2)}, u32[]{:S(2)}) collective-permute-start(bf16[1,2,1792]{2,0,1:T(2,128)(2,1)S(1)} %get-tuple-element.14), channel_id=1, source_target_pairs={{0,8},{1,9},{2,10},{3,11},{4,12},{5,13},{6,14},{7,15},{8,0},{9,1},... | collective-permute-start | bytes 21512 | tf_op jit(solution)/shard_map/ppermute | solution.py:84
  13.7 1.8 %collective-permute-start.6 = (bf16[1,2,1792]{2,0,1:T(2,128)(2,1)S(1)}, bf16[1,2,1792]{2,0,1:T(2,128)(2,1)S(1)}, u32[]{:S(2)}, u32[]{:S(2)}) collective-permute-start(bf16[1,2,1792]{2,0,1:T(2,128)(2,1)S(1)} %get-tuple-element.15), channel_id=1, source_target_pairs={{0,7},{1,6},{2,5},{3,4},{4,3},{5,2},{6,1},{7,0},{8,15},{9,14},{10,... | collective-permute-start | bytes 21512 | tf_op jit(solution)/shard_map/ppermute | solution.py:84
  15.5 1.4 %collective-permute-start.5 = (bf16[1,2,1792]{2,0,1:T(2,128)(2,1)S(1)}, bf16[1,2,1792]{2,0,1:T(2,128)(2,1)S(1)}, u32[]{:S(2)}, u32[]{:S(2)}) collective-permute-start(bf16[1,2,1792]{2,0,1:T(2,128)(2,1)S(1)} %get-tuple-element.16), channel_id=1, source_target_pairs={{0,6},{1,7},{2,4},{3,5},{4,2},{5,3},{6,0},{7,1},{8,14},{9,15},{10,... | collective-permute-start | bytes 21512 | tf_op jit(solution)/shard_map/ppermute | solution.py:84
  16.9 0.7 %collective-permute-start.4 = (bf16[1,2,1792]{2,0,1:T(2,128)(2,1)S(1)}, bf16[1,2,1792]{2,0,1:T(2,128)(2,1)S(1)}, u32[]{:S(2)}, u32[]{:S(2)}) collective-permute-start(bf16[1,2,1792]{2,0,1:T(2,128)(2,1)S(1)} %get-tuple-element.17), channel_id=1, source_target_pairs={{0,5},{1,4},{2,7},{3,6},{4,1},{5,0},{6,3},{7,2},{8,13},{9,12},{10,... | collective-permute-start | bytes 21512 | tf_op jit(solution)/shard_map/ppermute | solution.py:84
  17.7 0.9 %collective-permute-start.3 = (bf16[1,2,1792]{2,0,1:T(2,128)(2,1)S(1)}, bf16[1,2,1792]{2,0,1:T(2,128)(2,1)S(1)}, u32[]{:S(2)}, u32[]{:S(2)}) collective-permute-start(bf16[1,2,1792]{2,0,1:T(2,128)(2,1)S(1)} %get-tuple-element.18), channel_id=1, source_target_pairs={{0,4},{1,5},{2,6},{3,7},{4,0},{5,1},{6,2},{7,3},{8,12},{9,13},{10,... | collective-permute-start | bytes 21512 | tf_op jit(solution)/shard_map/ppermute | solution.py:84
  18.6 0.0 collective-permute-done.7
  18.6 0.3 collective-permute-start.2
  18.9 1.5 %collective-permute-start.1 = (bf16[1,2,1792]{2,0,1:T(2,128)(2,1)S(1)}, bf16[1,2,1792]{2,0,1:T(2,128)(2,1)S(1)}, u32[]{:S(2)}, u32[]{:S(2)}) collective-permute-start(bf16[1,2,1792]{2,0,1:T(2,128)(2,1)S(1)} %get-tuple-element.20), channel_id=1, source_target_pairs={{0,2},{1,3},{2,0},{3,1},{4,6},{5,7},{6,4},{7,5},{8,10},{9,11},{10,... | collective-permute-start | bytes 21512 | tf_op jit(solution)/shard_map/ppermute | solution.py:84
  20.4 0.0 collective-permute-start
  20.4 1.4 %collective-permute-start.12 = (bf16[1,2,1792]{2,0,1:T(2,128)(2,1)S(1)}, bf16[1,2,1792]{2,0,1:T(2,128)(2,1)S(1)}, u32[]{:S(2)}, u32[]{:S(2)}) collective-permute-start(bf16[1,2,1792]{2,0,1:T(2,128)(2,1)S(1)} %get-tuple-element.9), channel_id=1, source_target_pairs={{0,13},{1,12},{2,15},{3,14},{4,9},{5,8},{6,11},{7,10},{8,5},{9,4},... | collective-permute-start | bytes 21512 | tf_op jit(solution)/shard_map/ppermute | solution.py:84
  21.9 1.3 %collective-permute-start.10 = (bf16[1,2,1792]{2,0,1:T(2,128)(2,1)S(1)}, bf16[1,2,1792]{2,0,1:T(2,128)(2,1)S(1)}, u32[]{:S(2)}, u32[]{:S(2)}) collective-permute-start(bf16[1,2,1792]{2,0,1:T(2,128)(2,1)S(1)} %get-tuple-element.11), channel_id=1, source_target_pairs={{0,11},{1,10},{2,9},{3,8},{4,15},{5,14},{6,13},{7,12},{8,3},{9,2},... | collective-permute-start | bytes 21512 | tf_op jit(solution)/shard_map/ppermute | solution.py:84
  23.2 1.3 %collective-permute-start.11 = (bf16[1,2,1792]{2,0,1:T(2,128)(2,1)S(1)}, bf16[1,2,1792]{2,0,1:T(2,128)(2,1)S(1)}, u32[]{:S(2)}, u32[]{:S(2)}) collective-permute-start(bf16[1,2,1792]{2,0,1:T(2,128)(2,1)S(1)} %get-tuple-element.10), channel_id=1, source_target_pairs={{0,12},{1,13},{2,14},{3,15},{4,8},{5,9},{6,10},{7,11},{8,4},{9,5},... | collective-permute-start | bytes 21512 | tf_op jit(solution)/shard_map/ppermute | solution.py:84
  24.5 3.5 %collective-permute-start.13 = (bf16[1,2,1792]{2,0,1:T(2,128)(2,1)S(1)}, bf16[1,2,1792]{2,0,1:T(2,128)(2,1)S(1)}, u32[]{:S(2)}, u32[]{:S(2)}) collective-permute-start(bf16[1,2,1792]{2,0,1:T(2,128)(2,1)S(1)} %get-tuple-element.8), channel_id=1, source_target_pairs={{0,14},{1,15},{2,12},{3,13},{4,10},{5,11},{6,8},{7,9},{8,6},{9,7},... | collective-permute-start | bytes 21512 | tf_op jit(solution)/shard_map/ppermute | solution.py:84
  28.0 0.5 collective-permute-start.14
  28.5 0.1 dynamic_update_slice.48
  28.6 0.1 dynamic_update_slice.49
  28.8 0.1 dynamic_update_slice.50
  28.9 0.1 dynamic_update_slice.51
  29.0 0.1 dynamic_update_slice.52
  29.2 0.1 dynamic_update_slice.53
  29.3 0.1 dynamic_update_slice.54
  29.5 0.1 dynamic_update_slice.55
  29.6 0.1 dynamic_update_slice.56
  29.7 0.1 dynamic_update_slice.57
  29.9 0.1 dynamic_update_slice.58
  30.0 0.1 dynamic_update_slice.59
  30.2 0.1 dynamic_update_slice.60
  30.3 0.1 dynamic_update_slice.61
  30.5 0.5 collective-permute-done.13
  30.9 0.1 dynamic_update_slice.62
  31.0 2.9 %collective-permute-done.14 = bf16[1,2,1792]{2,0,1:T(2,128)(2,1)S(1)} collective-permute-done((bf16[1,2,1792]{2,0,1:T(2,128)(2,1)S(1)}, bf16[1,2,1792]{2,0,1:T(2,128)(2,1)S(1)}, u32[]{:S(2)}, u32[]{:S(2)}) %collective-permute-start.14) | collective-permute-done | bytes 7200 | tf_op jit(solution)/shard_map/ppermute | solution.py:84
  33.9 0.1 dynamic_update_slice.63
  34.0 0.2 collective-permute-start.15
  34.2 1.2 %collective-permute-done.15 = bf16[16,2,1792]{2,0,1:T(8,128)(2,1)S(1)} collective-permute-done((bf16[16,2,1792]{2,0,1:T(8,128)(2,1)S(1)}, bf16[16,2,1792]{2,0,1:T(8,128)(2,1)S(1)}, u32[]{:S(2)}, u32[]{:S(2)}) %collective-permute-start.15) | collective-permute-done | bytes 114720 | tf_op jit(solution)/shard_map/ppermute | solution.py:17
  35.4 2.8 %fusion.8 = f32[16,1,2,512]{3,0,2,1:T(8,128)S(1)} fusion(bf16[1,3584,512]{2,1,0:T(8,128)(2,1)} %param.9, bf16[16,2,1792]{2,0,1:T(8,128)(2,1)S(1)} %get-tuple-element.6, bf16[16,2,1792]{2,0,1:T(8,128)(2,1)S(1)} %get-tuple-element.5), kind=kOutput, calls=%fused_computation.12 | convolution fusion | flops 117899264 | bytes 3964928 | tf_op jit(solution)/shard_map/secd,edf->secf/dot_general | solution.py:26
  38.2 0.0 copy-start.2
  38.2 4.6 %fusion = f32[16,2,3584]{2,0,1:T(8,128)S(1)} fusion(bf16[1,512,3584]{2,1,0:T(8,128)(2,1)} %param.11, f32[16,1,2,512]{3,0,2,1:T(8,128)S(1)} %fusion.8, bf16[1,3584,512]{2,1,0:T(8,128)(2,1)} %param.10, bf16[16,2,1792]{2,0,1:T(8,128)(2,1)S(1)} %get-tuple-element.6, bf16[16,2,1792]{2,0,1:T(8,128)(2,1)S(1)} %get-tuple-element.5), kind=kOutput, calls=%fused_computation.4 | convolution fusion | flops 235438080 | bytes 8093696 | tf_op jit(solution)/shard_map/secf,efd->secd/dot_general | solution.py:29
  42.9 0.2 collective-permute-start.16
  43.1 1.3 %collective-permute-done.16 = f32[16,2,1792]{2,0,1:T(8,128)S(1)} collective-permute-done((f32[16,2,1792]{2,0,1:T(8,128)S(1)}, f32[16,2,1792]{2,0,1:T(8,128)S(1)}, u32[]{:S(2)}, u32[]{:S(2)}) %collective-permute-start.16) | collective-permute-done | bytes 229408 | tf_op jit(solution)/shard_map/ppermute | solution.py:17
  44.4 0.1 add_convert_fusion
  44.5 0.7 %copy.21 = bf16[16,2,1792]{2,1,0:T(2,128)(2,1)} copy(bf16[16,2,1792]{2,0,1:T(8,128)(2,1)S(1)} %add_convert_fusion) | data formatting | bytes 229376 | tf_op jit(solution)/shard_map/convert_element_type | solution.py:46
  45.2 3.5 %all-to-all-start = ((bf16[16,2,1792]{2,1,0:T(2,128)(2,1)}), bf16[16,2,1792]{2,1,0:T(2,128)(2,1)S(1)}, u32[]{:S(2)}, u32[]{:S(2)}) async-start(bf16[16,2,1792]{2,1,0:T(2,128)(2,1)} %copy.21), calls=%async_computation | async-start | bytes 229376 | tf_op jit(solution)/shard_map/all_to_all | solution.py:47
  48.8 0.1 copy.23
  48.9 7.5 %all-to-all-done = bf16[16,2,1792]{2,1,0:T(2,128)(2,1)S(1)} async-done(((bf16[16,2,1792]{2,1,0:T(2,128)(2,1)}), bf16[16,2,1792]{2,1,0:T(2,128)(2,1)S(1)}, u32[]{:S(2)}, u32[]{:S(2)}) %all-to-all-start) | async-done | bytes 114720 | tf_op jit(solution)/shard_map/all_to_all | solution.py:47
  56.3 0.1 copy.29
  56.4 0.1 reshape.142
  56.5 4.1 %gather_fusion.1 = bf16[256,3584]{1,0:T(8,128)(2,1)S(1)} fusion(bf16[8,2,3584]{2,1,0:T(2,128)(2,1)S(1)} %reshape.142, s32[256]{0:T(256)S(1)} %bitcast.69), kind=kCustom, calls=%fused_computation.1 | custom fusion | bytes 3672064 | tf_op jit(solution)/shard_map/gather | solution.py:92
  60.6 0.6 %fusion.6 = bf16[32,1,3584]{2,1,0:T(2,128)(2,1)S(1)} fusion(bf16[32,8,1]{1,2,0:T(2,128)(2,1)S(1)} %copy.23, bf16[256,3584]{1,0:T(8,128)(2,1)S(1)} %gather_fusion.1), kind=kOutput, calls=%fused_computation.10 | convolution fusion | flops 1835008 | bytes 2064896 | tf_op jit(solution)/shard_map/tk,tkd->td/dot_general | solution.py:98
  61.3 0.7 %copy.28 = bf16[32,1,3584]{2,0,1:T(8,128)(2,1)} copy(bf16[32,1,3584]{2,1,0:T(2,128)(2,1)S(1)} %fusion.6) | data formatting | bytes 458752 | tf_op jit(solution)/shard_map/tk,tkd->td/dot_general | solution.py:98
  (32 shorter events, 0.3 us)
Async XLA Ops:
  0.0 5.2 %copy-start = (bf16[32,3584]{1,0:T(8,128)(2,1)S(1)}, bf16[32,3584]{1,0:T(8,128)(2,1)}, u32[]{:S(2)}) copy-start(bf16[32,3584]{1,0:T(8,128)(2,1)} %param.6) | copy-start | bytes 688132
  6.5 10.4 %collective-permute-start.9 = (bf16[1,2,1792]{2,0,1:T(2,128)(2,1)S(1)}, bf16[1,2,1792]{2,0,1:T(2,128)(2,1)S(1)}, u32[]{:S(2)}, u32[]{:S(2)}) collective-permute-start(bf16[1,2,1792]{2,0,1:T(2,128)(2,1)S(1)} %get-tuple-element.12), channel_id=1, source_target_pairs={{0,10},{1,11},{2,8},{3,9},{4,14},{5,15},{6,12},{7,13},{8,2},{9,3},... | collective-permute-start | bytes 21512 | tf_op jit(solution)/shard_map/ppermute | solution.py:84
  11.6 6.0 %collective-permute-start.8 = (bf16[1,2,1792]{2,0,1:T(2,128)(2,1)S(1)}, bf16[1,2,1792]{2,0,1:T(2,128)(2,1)S(1)}, u32[]{:S(2)}, u32[]{:S(2)}) collective-permute-start(bf16[1,2,1792]{2,0,1:T(2,128)(2,1)S(1)} %get-tuple-element.13), channel_id=1, source_target_pairs={{0,9},{1,8},{2,11},{3,10},{4,13},{5,12},{6,15},{7,14},{8,1},{9,0},... | collective-permute-start | bytes 21512 | tf_op jit(solution)/shard_map/ppermute | solution.py:84
  11.6 6.9 %collective-permute-start.7 = (bf16[1,2,1792]{2,0,1:T(2,128)(2,1)S(1)}, bf16[1,2,1792]{2,0,1:T(2,128)(2,1)S(1)}, u32[]{:S(2)}, u32[]{:S(2)}) collective-permute-start(bf16[1,2,1792]{2,0,1:T(2,128)(2,1)S(1)} %get-tuple-element.14), channel_id=1, source_target_pairs={{0,8},{1,9},{2,10},{3,11},{4,12},{5,13},{6,14},{7,15},{8,0},{9,1},... | collective-permute-start | bytes 21512 | tf_op jit(solution)/shard_map/ppermute | solution.py:84
  13.7 5.2 %collective-permute-start.6 = (bf16[1,2,1792]{2,0,1:T(2,128)(2,1)S(1)}, bf16[1,2,1792]{2,0,1:T(2,128)(2,1)S(1)}, u32[]{:S(2)}, u32[]{:S(2)}) collective-permute-start(bf16[1,2,1792]{2,0,1:T(2,128)(2,1)S(1)} %get-tuple-element.15), channel_id=1, source_target_pairs={{0,7},{1,6},{2,5},{3,4},{4,3},{5,2},{6,1},{7,0},{8,15},{9,14},{10,... | collective-permute-start | bytes 21512 | tf_op jit(solution)/shard_map/ppermute | solution.py:84
  15.5 4.9 %collective-permute-start.5 = (bf16[1,2,1792]{2,0,1:T(2,128)(2,1)S(1)}, bf16[1,2,1792]{2,0,1:T(2,128)(2,1)S(1)}, u32[]{:S(2)}, u32[]{:S(2)}) collective-permute-start(bf16[1,2,1792]{2,0,1:T(2,128)(2,1)S(1)} %get-tuple-element.16), channel_id=1, source_target_pairs={{0,6},{1,7},{2,4},{3,5},{4,2},{5,3},{6,0},{7,1},{8,14},{9,15},{10,... | collective-permute-start | bytes 21512 | tf_op jit(solution)/shard_map/ppermute | solution.py:84
  16.9 3.5 %collective-permute-start.4 = (bf16[1,2,1792]{2,0,1:T(2,128)(2,1)S(1)}, bf16[1,2,1792]{2,0,1:T(2,128)(2,1)S(1)}, u32[]{:S(2)}, u32[]{:S(2)}) collective-permute-start(bf16[1,2,1792]{2,0,1:T(2,128)(2,1)S(1)} %get-tuple-element.17), channel_id=1, source_target_pairs={{0,5},{1,4},{2,7},{3,6},{4,1},{5,0},{6,3},{7,2},{8,13},{9,12},{10,... | collective-permute-start | bytes 21512 | tf_op jit(solution)/shard_map/ppermute | solution.py:84
  17.7 4.2 %collective-permute-start.3 = (bf16[1,2,1792]{2,0,1:T(2,128)(2,1)S(1)}, bf16[1,2,1792]{2,0,1:T(2,128)(2,1)S(1)}, u32[]{:S(2)}, u32[]{:S(2)}) collective-permute-start(bf16[1,2,1792]{2,0,1:T(2,128)(2,1)S(1)} %get-tuple-element.18), channel_id=1, source_target_pairs={{0,4},{1,5},{2,6},{3,7},{4,0},{5,1},{6,2},{7,3},{8,12},{9,13},{10,... | collective-permute-start | bytes 21512 | tf_op jit(solution)/shard_map/ppermute | solution.py:84
  18.6 4.6 %collective-permute-start.2 = (bf16[1,2,1792]{2,0,1:T(2,128)(2,1)S(1)}, bf16[1,2,1792]{2,0,1:T(2,128)(2,1)S(1)}, u32[]{:S(2)}, u32[]{:S(2)}) collective-permute-start(bf16[1,2,1792]{2,0,1:T(2,128)(2,1)S(1)} %get-tuple-element.19), channel_id=1, source_target_pairs={{0,3},{1,2},{2,1},{3,0},{4,7},{5,6},{6,5},{7,4},{8,11},{9,10},{10,... | collective-permute-start | bytes 21512 | tf_op jit(solution)/shard_map/ppermute | solution.py:84
  18.9 5.6 %collective-permute-start.1 = (bf16[1,2,1792]{2,0,1:T(2,128)(2,1)S(1)}, bf16[1,2,1792]{2,0,1:T(2,128)(2,1)S(1)}, u32[]{:S(2)}, u32[]{:S(2)}) collective-permute-start(bf16[1,2,1792]{2,0,1:T(2,128)(2,1)S(1)} %get-tuple-element.20), channel_id=1, source_target_pairs={{0,2},{1,3},{2,0},{3,1},{4,6},{5,7},{6,4},{7,5},{8,10},{9,11},{10,... | collective-permute-start | bytes 21512 | tf_op jit(solution)/shard_map/ppermute | solution.py:84
  20.4 7.6 %collective-permute-start = (bf16[1,2,1792]{2,0,1:T(2,128)(2,1)S(1)}, bf16[1,2,1792]{2,0,1:T(2,128)(2,1)S(1)}, u32[]{:S(2)}, u32[]{:S(2)}) collective-permute-start(bf16[1,2,1792]{2,0,1:T(2,128)(2,1)S(1)} %get-tuple-element.21), channel_id=1, source_target_pairs={{0,1},{1,0},{2,3},{3,2},{4,5},{5,4},{6,7},{7,6},{8,9},{9,8},{10,11... | collective-permute-start | bytes 21512 | tf_op jit(solution)/shard_map/ppermute | solution.py:84
  20.4 9.9 %collective-permute-start.12 = (bf16[1,2,1792]{2,0,1:T(2,128)(2,1)S(1)}, bf16[1,2,1792]{2,0,1:T(2,128)(2,1)S(1)}, u32[]{:S(2)}, u32[]{:S(2)}) collective-permute-start(bf16[1,2,1792]{2,0,1:T(2,128)(2,1)S(1)} %get-tuple-element.9), channel_id=1, source_target_pairs={{0,13},{1,12},{2,15},{3,14},{4,9},{5,8},{6,11},{7,10},{8,5},{9,4},... | collective-permute-start | bytes 21512 | tf_op jit(solution)/shard_map/ppermute | solution.py:84
  21.9 8.1 %collective-permute-start.10 = (bf16[1,2,1792]{2,0,1:T(2,128)(2,1)S(1)}, bf16[1,2,1792]{2,0,1:T(2,128)(2,1)S(1)}, u32[]{:S(2)}, u32[]{:S(2)}) collective-permute-start(bf16[1,2,1792]{2,0,1:T(2,128)(2,1)S(1)} %get-tuple-element.11), channel_id=1, source_target_pairs={{0,11},{1,10},{2,9},{3,8},{4,15},{5,14},{6,13},{7,12},{8,3},{9,2},... | collective-permute-start | bytes 21512 | tf_op jit(solution)/shard_map/ppermute | solution.py:84
  23.2 7.0 %collective-permute-start.11 = (bf16[1,2,1792]{2,0,1:T(2,128)(2,1)S(1)}, bf16[1,2,1792]{2,0,1:T(2,128)(2,1)S(1)}, u32[]{:S(2)}, u32[]{:S(2)}) collective-permute-start(bf16[1,2,1792]{2,0,1:T(2,128)(2,1)S(1)} %get-tuple-element.10), channel_id=1, source_target_pairs={{0,12},{1,13},{2,14},{3,15},{4,8},{5,9},{6,10},{7,11},{8,4},{9,5},... | collective-permute-start | bytes 21512 | tf_op jit(solution)/shard_map/ppermute | solution.py:84
  24.5 6.4 %collective-permute-start.13 = (bf16[1,2,1792]{2,0,1:T(2,128)(2,1)S(1)}, bf16[1,2,1792]{2,0,1:T(2,128)(2,1)S(1)}, u32[]{:S(2)}, u32[]{:S(2)}) collective-permute-start(bf16[1,2,1792]{2,0,1:T(2,128)(2,1)S(1)} %get-tuple-element.8), channel_id=1, source_target_pairs={{0,14},{1,15},{2,12},{3,13},{4,10},{5,11},{6,8},{7,9},{8,6},{9,7},... | collective-permute-start | bytes 21512 | tf_op jit(solution)/shard_map/ppermute | solution.py:84
  28.0 5.9 %collective-permute-start.14 = (bf16[1,2,1792]{2,0,1:T(2,128)(2,1)S(1)}, bf16[1,2,1792]{2,0,1:T(2,128)(2,1)S(1)}, u32[]{:S(2)}, u32[]{:S(2)}) collective-permute-start(bf16[1,2,1792]{2,0,1:T(2,128)(2,1)S(1)} %get-tuple-element.7), channel_id=1, source_target_pairs={{0,15},{1,14},{2,13},{3,12},{4,11},{5,10},{6,9},{7,8},{8,7},{9,6},... | collective-permute-start | bytes 21512 | tf_op jit(solution)/shard_map/ppermute | solution.py:84
  34.0 1.4 %collective-permute-start.15 = (bf16[16,2,1792]{2,0,1:T(8,128)(2,1)S(1)}, bf16[16,2,1792]{2,0,1:T(8,128)(2,1)S(1)}, u32[]{:S(2)}, u32[]{:S(2)}) collective-permute-start(bf16[16,2,1792]{2,0,1:T(8,128)(2,1)S(1)} %dynamic_update_slice.63), channel_id=1, source_target_pairs={{0,1},{1,0},{2,3},{3,2},{4,5},{5,4},{6,7},{7,6},{8,9},{9,8},{10,11... | collective-permute-start | bytes 344072 | tf_op jit(solution)/shard_map/ppermute | solution.py:17
  38.2 10.5 %copy-start.1 = (s32[32,8]{0,1:T(8,128)S(1)}, s32[32,8]{0,1:T(8,128)}, u32[]{:S(2)}) copy-start(s32[32,8]{0,1:T(8,128)} %param.7) | copy-start | bytes 3076
  38.2 10.5 %copy-start.2 = (s32[32,8]{0,1:T(8,128)S(1)}, s32[32,8]{0,1:T(8,128)}, u32[]{:S(2)}) copy-start(s32[32,8]{0,1:T(8,128)} %param.8) | copy-start | bytes 3076
  42.9 1.6 %collective-permute-start.16 = (f32[16,2,1792]{2,0,1:T(8,128)S(1)}, f32[16,2,1792]{2,0,1:T(8,128)S(1)}, u32[]{:S(2)}, u32[]{:S(2)}) collective-permute-start(f32[16,2,1792]{2,0,1:T(8,128)S(1)} %slice_select_fusion), channel_id=1, source_target_pairs={{0,1},{1,0},{2,3},{3,2},{4,5},{5,4},{6,7},{7,6},{8,9},{9,8},{10,11... | collective-permute-start | bytes 688136 | tf_op jit(solution)/shard_map/ppermute | solution.py:17
  45.2 11.1 %all-to-all-start = ((bf16[16,2,1792]{2,1,0:T(2,128)(2,1)}), bf16[16,2,1792]{2,1,0:T(2,128)(2,1)S(1)}, u32[]{:S(2)}, u32[]{:S(2)}) async-start(bf16[16,2,1792]{2,1,0:T(2,128)(2,1)} %copy.21), calls=%async_computation | async-start | bytes 229376 | tf_op jit(solution)/shard_map/all_to_all | solution.py:47
